TPU v7x, 32 devices: a whole 2x2x4 slice. The times are simulated.
32 devices in a mesh: lat: 2 (over core), prop: 16 (over z, y, x).
Axes of the slice: x: 2, y: 2, z: 4, core: 2. Of those that a mesh axis runs over, the one named last changes fastest.
Arguments:
- right_side: float32 [2, 3, 16, 64, 4, 128], P(None, None, None, 'prop', 'lat'), may hold values from -30 to 30
- start_field: float32 [2, 3, 16, 64, 4, 128], P(None, None, None, 'prop', 'lat'), may hold values from -1.75 to 1.75
- region: int32 [64, 4, 128], P('prop', 'lat'), may hold values from 0 to 7
- core_mask: int32 [64, 4, 128], P('prop', 'lat'), may hold values 0 or 1
- intensity: float32 [64, 4, 128], P('prop', 'lat'), may hold values from 0 to 4
- eps_lin: float32 [8], replicated, may hold values from 1 to 12
- eps_loss: float32 [8], replicated, may hold values from 0.1 to 3
- kerr_coef: float32 [8], replicated, may hold values from 0.2 to 1
Outputs:
- new_field: float32 [2, 3, 16, 64, 4, 128], P(None, None, None, 'prop', 'lat')
All inputs are finite; a program needn't handle non-finite values. No bound on the sum of `core_mask` on one device may be relied on, other than what follows from the above.
Results may differ from a plain program's by a relative error of at most 0.00002.
Values sent between devices are 32-bit elements; how exact they have to be, the bound alone decides.
A program may use at most 64 MiB of HBM per device.

v0:
```python
import jax
import jax.numpy as jnp
from jax import lax
from jax.sharding import PartitionSpec as P

wave_sq = 0.25
wave_shift = 0.02
loss_gain = 3.2
tiny = 1e-06


def extended(array, sides, width):
    for axis, dim in sides:
        size, length = (lax.axis_size(axis), array.shape[dim])
        up = [(i, (i + 1) % size) for i in range(size - 1)]
        down = [(j, i) for i, j in up]
        last = lax.slice_in_dim(array, length - width, length, axis=dim)
        first = lax.slice_in_dim(array, 0, width, axis=dim)
        before = lax.ppermute(last, axis, up)
        after = lax.ppermute(first, axis, down)
        array = jnp.concatenate([before, array, after], axis=dim)
    return array


def trimmed(values, direction):
    selector = [slice(None)] * (values.ndim - 3) + [slice(0, -1)] * 3
    if direction is not None:
        selector[values.ndim + direction] = slice(1, None)
    return values[tuple(selector)]


def advance(values, direction):
    return trimmed(values, direction) - trimmed(values, None)


def upper(values, direction):
    selector = [slice(None)] * (values.ndim - 3) + [slice(1, None)] * 3
    if direction is not None:
        selector[values.ndim + direction] = slice(0, -1)
    return values[tuple(selector)]


def retreat(values, direction):
    return upper(values, None) - upper(values, direction)


def curl_twice(padded):
    field_x = padded[:, 0]
    field_y = padded[:, 1]
    field_z = padded[:, 2]
    magnet_x = advance(field_z, -1) - advance(field_y, -3)
    magnet_y = advance(field_x, -3) - advance(field_z, -2)
    magnet_z = advance(field_y, -2) - advance(field_x, -1)
    result_x = retreat(magnet_z, -1) - retreat(magnet_y, -3)
    result_y = retreat(magnet_x, -3) - retreat(magnet_z, -2)
    result_z = retreat(magnet_y, -2) - retreat(magnet_x, -1)
    return jnp.stack([result_x, result_y, result_z], axis=1)


def apply_operator(values, padded, perm_real, perm_imag):
    curled = curl_twice(padded)
    real_part = values[0]
    imag_part = values[1]
    out_real = curled[0] - wave_sq * (perm_real * real_part - perm_imag * imag_part)
    out_imag = curled[1] - wave_sq * (perm_real * imag_part + perm_imag * real_part)
    return jnp.stack([out_real, out_imag])


def ascend(gain_real, gain_imag, forward_value, behind):
    return jnp.stack(
        [
            forward_value[0] + gain_real * behind[0] - gain_imag * behind[1],
            forward_value[1] + gain_real * behind[1] + gain_imag * behind[0],
        ]
    )


def solve_batched(line_data, diag_real, diag_imag):
    depth = line_data.shape[3]
    lines_count = line_data.shape[4] * line_data.shape[5]
    moved = jnp.moveaxis(line_data, 3, 0)
    moved_shape = moved.shape
    rows = moved.reshape((depth, 2, -1))
    repeats = rows.shape[2] // lines_count
    plane_real = diag_real.reshape((depth, lines_count))
    plane_imag = diag_imag.reshape((depth, lines_count))
    unroll_count = min(16, depth)

    def gain_step(carried, element):
        gain_real, gain_imag = carried
        diag_now_real, diag_now_imag = element
        denom_real = diag_now_real - gain_real
        denom_imag = diag_now_imag - gain_imag
        magnitude = denom_real * denom_real + denom_imag * denom_imag
        new_real = denom_real / magnitude
        new_imag = -denom_imag / magnitude
        return ((new_real, new_imag), (new_real, new_imag))

    zero_line = jnp.zeros((lines_count,), jnp.float32)
    unused, (gains_real, gains_imag) = lax.scan(
        gain_step, (zero_line, zero_line), (plane_real, plane_imag), unroll=unroll_count
    )
    wide_real = jnp.tile(gains_real, (1, repeats))
    wide_imag = jnp.tile(gains_imag, (1, repeats))

    def front_step(previous, element):
        gain_real, gain_imag, source = element
        sum_real = source[0] + previous[0]
        sum_imag = source[1] + previous[1]
        updated = jnp.stack(
            [
                gain_real * sum_real - gain_imag * sum_imag,
                gain_real * sum_imag + gain_imag * sum_real,
            ]
        )
        return (updated, updated)

    unused, fronts = lax.scan(
        front_step, jnp.zeros_like(rows[0]), (wide_real, wide_imag, rows), unroll=unroll_count
    )

    def back_step(behind, element):
        gain_real, gain_imag, forward_value = element
        new_value = ascend(gain_real, gain_imag, forward_value, behind)
        return (new_value, new_value)

    unused, values = lax.scan(
        back_step,
        jnp.zeros_like(rows[0]),
        (wide_real, wide_imag, fronts),
        reverse=True,
        unroll=unroll_count,
    )
    return jnp.moveaxis(values.reshape(moved_shape), 0, 3)


def per_device(right_side, start_field, region, core_mask, intensity, eps_lin, eps_loss, kerr_coef):
    levels = jnp.arange(eps_lin.shape[0], dtype=jnp.int32)
    onehot = (region[None] == levels[:, None, None, None]).astype(jnp.float32)
    lin_cell = jnp.sum(onehot * eps_lin[:, None, None, None], axis=0)
    loss_cell = jnp.sum(onehot * eps_loss[:, None, None, None], axis=0)
    kerr_cell = jnp.sum(onehot * kerr_coef[:, None, None, None], axis=0)
    perm_real = lin_cell + core_mask.astype(jnp.float32) * kerr_cell * intensity
    planes = right_side.shape[3]
    total_planes = planes * lax.axis_size("prop")
    diag_real = 2.0 - wave_shift * perm_real
    diag_imag = loss_gain / total_planes * loss_cell

    def operate(values):
        padded = extended(values, (("lat", 4), ("prop", 3)), 1)
        padded = jnp.pad(padded, ((0, 0), (0, 0), (0, 0), (0, 0), (0, 0), (1, 1)))
        return apply_operator(values, padded, perm_real, loss_cell)

    residual = right_side - operate(start_field)
    coeffs = jnp.stack([diag_real, diag_imag])
    line_diag = lax.all_to_all(coeffs, "prop", split_axis=3, concat_axis=1, tiled=True)
    solved = solve_batched(
        lax.all_to_all(residual, "prop", split_axis=5, concat_axis=3, tiled=True),
        line_diag[0],
        line_diag[1],
    )
    precond = lax.all_to_all(solved, "prop", split_axis=3, concat_axis=5, tiled=True)
    image_field = operate(precond)
    cross_sum = jnp.sum(residual * image_field, axis=(0, 1, 3, 4, 5))
    self_sum = jnp.sum(image_field * image_field, axis=(0, 1, 3, 4, 5))
    totals = lax.psum((cross_sum, self_sum), ("lat", "prop"))
    step_size = totals[0] / (totals[1] + tiny)
    return start_field + step_size[None, None, :, None, None, None] * precond


def solution(mesh):
    placed = (
        P(None, None, None, "prop", "lat", None),
        P(None, None, None, "prop", "lat", None),
        P("prop", "lat", None),
        P("prop", "lat", None),
        P("prop", "lat", None),
        P(),
        P(),
        P(),
    )
    return jax.shard_map(
        per_device,
        mesh=mesh,
        in_specs=placed,
        out_specs=P(None, None, None, "prop", "lat", None),
        check_vma=False,
    )
```

profile of v0, /device:TPU:0, one launch (start us, length us, event | category | flops | bytes accessed | tf_op | source)
XLA Modules:
  0.0 232.1 jit_solution(9379006360073458968)
XLA Ops:
  0.0 1.1 copy.262
  1.2 2.4 %collective-permute-start = (f32[2,3,16,4,1,128]{5,2,4,3,1,0:T(8,128)S(1)}, f32[2,3,16,4,1,128]{5,2,4,3,1,0:T(8,128)S(1)}, u32[]{:S(2)}, u32[]{:S(2)}) collective-permute-start(f32[2,3,16,4,1,128]{5,2,4,3,1,0:T(8,128)S(1)} %get-tuple-element.468), channel_id=1, source_target_pairs={{0,16},{1,17},{2,18},{3,19},{4,20},{5,21},{6,22},{7,23},{8,24},{9,... | collective-permute-start | bytes 589832 | tf_op jit(solution)/shard_map/ppermute | solution.py:19
  6.3 7.7 %all-to-all-start = ((f32[16,1,128]{2,1,0:T(1,128)}), f32[16,1,128]{2,1,0:T(1,128)S(1)}, u32[]{:S(2)}, u32[]{:S(2)}) async-start(f32[16,1,128]{2,1,0:T(1,128)} %reshape.3988), calls=%async_computation | async-start | bytes 16384 | tf_op jit(solution)/shard_map/all_to_all | solution.py:156
  14.0 1.3 collective-permute-start.1
  15.4 5.9 %all-to-all-done = f32[16,1,128]{2,1,0:T(1,128)S(1)} async-done(((f32[16,1,128]{2,1,0:T(1,128)}), f32[16,1,128]{2,1,0:T(1,128)S(1)}, u32[]{:S(2)}, u32[]{:S(2)}) %all-to-all-start) | async-done | bytes 8224 | tf_op jit(solution)/shard_map/all_to_all | solution.py:156
  23.6 2.5 %collective-permute-start.2 = (f32[2,3,16,1,4,128]{5,2,4,3,1,0:T(8,128)S(1)}, f32[2,3,16,1,4,128]{5,2,4,3,1,0:T(8,128)S(1)}, u32[]{:S(2)}, u32[]{:S(2)}) collective-permute-start(f32[2,3,16,1,4,128]{5,2,4,3,1,0:T(8,128)S(1)} %get-tuple-element.459), channel_id=1, source_target_pairs={{0,1},{1,2},{2,3},{3,4},{4,5},{5,6},{6,7},{7,8},{8,9},{9,10},{10,1... | collective-permute-start | bytes 589832 | tf_op jit(solution)/shard_map/ppermute | solution.py:19
  26.1 1.3 collective-permute-start.3
  29.3 5.3 %collective-permute-done.3 = f32[2,3,16,1,4,128]{5,2,4,3,1,0:T(8,128)S(1)} collective-permute-done((f32[2,3,16,1,4,128]{5,2,4,3,1,0:T(8,128)S(1)}, f32[2,3,16,1,4,128]{5,2,4,3,1,0:T(8,128)S(1)}, u32[]{:S(2)}, u32[]{:S(2)}) %collective-permute-start.3) | collective-permute-done | bytes 196640 | tf_op jit(solution)/shard_map/ppermute | solution.py:20
  37.2 2.2 copy.238
  39.4 4.9 %reshape.3990 = f32[16,1,6144]{2,1,0:T(1,128)} reshape(f32[128,2,3,4,2,16]{5,4,3,2,1,0:T(2,128)S(1)} %bitcast.1633) | data formatting | bytes 786432
  44.3 4.6 %all-to-all-start.1 = ((f32[16,1,6144]{2,1,0:T(1,128)}), f32[16,1,6144]{2,1,0:T(1,128)S(1)}, u32[]{:S(2)}, u32[]{:S(2)}) async-start(f32[16,1,6144]{2,1,0:T(1,128)} %reshape.3990), calls=%async_computation.1 | async-start | bytes 786432 | tf_op jit(solution)/shard_map/all_to_all | solution.py:158
  49.0 44.4 %while.47 = (s32[]{:T(128)}, f32[16]{0:T(128)S(1)}, f32[16]{0:T(128)S(1)}, f32[4,16,16]{2,1,0:T(8,128)S(1)}, f32[4,16,16]{2,1,0:T(8,128)S(1)}, /*index=5*/f32[4,...) while((s32[]{:T(128)}, f32[16]{0:T(128)S(1)}, ...), condition=%wide.region_4.5_spmd.clone, body=%wide.region_3.4_spmd.clone.sunk | while | flops 2482 | bytes 45483 | solution.py:100
  94.9 2.4 %reduce.1 = f32[16,6144]{1,0:T(8,128)} reduce(f32[16,1,6144]{2,1,0:T(1,128)S(1)} %all-to-all-done.1, f32[]{:T(128)} %broadcast.160), dimensions={1}, to_apply=%all_to_all.40.reduce_sub_computation | reduce | bytes 786436 | tf_op jit(solution)/shard_map/all_to_all | solution.py:158
  97.3 5.3 %reshape.3991 = f32[128,2,3,4,2,16]{5,4,3,2,1,0:T(2,128)S(1)} reshape(f32[16,6144]{1,0:T(8,128)} %reduce.1) | data formatting | bytes 786432
  102.5 0.9 copy.280
  103.9 2.3 copy.241
  106.2 2.5 %reshape_reshape.6 = f32[4,16,2,768]{1,0,3,2:T(4,128)S(1)} reshape(f32[64,2,3,16,2,8]{0,5,4,3,2,1:T(8,128)} %copy.241) | data formatting | bytes 786432 | tf_op jit(solution)/shard_map/reshape;reshape | solution.py:118
  108.7 2.1 copy.242
  110.9 9.7 %while.45 = (s32[]{:T(128)}, f32[2,768]{1,0:T(2,128)S(1)}, f32[4,16,2,768]{3,2,1,0:T(2,128)S(1)}, f32[4,16,768]{2,1,0:T(8,128)S(1)}, f32[4,16,2,768]{3,2,1,0:T(2...) while((s32[]{:T(128)}, f32[2,768]{1,0:T(2,128)S(1)}, ...), condition=%wide.region_6.7_spmd, body=%wide.region_5.6_spmd.sunk | while | flops 124432 | bytes 719313 | solution.py:118
  110.9 1.3 multiply_subtract_fusion.32
  113.4 1.3 multiply_subtract_fusion.32
  115.8 1.3 multiply_subtract_fusion.32
  118.2 1.3 multiply_subtract_fusion.32
  120.8 2.9 %while.46 = (s32[]{:T(128)}, f32[2,768]{1,0:T(2,128)S(1)}, f32[4,16,2,768]{3,2,1,0:T(2,128)S(1)}, f32[4,16,2,768]{3,2,1,0:T(2,128)S(1)}, f32[4,16,768]{2,1,0:T(8...) while((s32[]{:T(128)}, f32[2,768]{1,0:T(2,128)S(1)}, ...), condition=%wide.region_8.9_spmd, body=%wide.region_7.8_spmd.sunk | while | flops 122897 | bytes 713185 | solution.py:127
  124.5 2.8 %copy.243 = f32[4,16,2,768]{1,0,3,2:T(4,128)S(1)} copy(f32[4,16,2,768]{3,2,1,0:T(2,128)} %copy-done.8) | data formatting | bytes 786432 | tf_op jit(solution)/shard_map/while | solution.py:127
  127.3 2.2 reshape_reshape.7
  129.5 2.7 %copy.244 = f32[2,3,16,64,2,8]{2,5,4,1,0,3:T(8,128)S(1)} copy(f32[2,3,16,64,2,8]{3,5,4,2,1,0:T(8,128)} %bitcast.1638) | data formatting | bytes 786432 | tf_op jit(solution)/shard_map/transpose | solution.py:134
  132.2 1.1 reshape.3992
  133.3 18.0 %all_to_all.51 = f32[16,1,6144]{2,1,0:T(1,128)S(1)} all-to-all(f32[16,1,6144]{2,1,0:T(1,128)S(1)} %reshape.3992), channel_id=1, replica_groups=mesh['lat'=2,'prop'=16] {'prop'}, dimensions={0} | all-to-all | bytes 786432 | tf_op jit(solution)/shard_map/all_to_all | solution.py:162
  151.3 1.5 reduce.2
  152.9 1.1 reshape.3993
  153.9 2.1 copy.245
  156.6 2.3 copy.279
  158.9 1.9 fusion.385
  160.8 1.1 copy.249
  161.9 2.7 %copy.247 = f32[2,3,16,4,1,128]{5,2,4,3,1,0:T(8,128)} copy(f32[2,3,16,4,1,128]{2,5,4,3,1,0:T(8,128)} %get-tuple-element.439) | data formatting | bytes 393216 | tf_op jit(solution)/shard_map/slice | solution.py:17
  164.6 2.0 collective-permute-start.4
  166.5 2.5 %copy.248 = f32[2,3,16,4,1,128]{5,2,4,3,1,0:T(8,128)} copy(f32[2,3,16,4,1,128]{2,5,4,3,1,0:T(8,128)} %get-tuple-element.440) | data formatting | bytes 393216 | tf_op jit(solution)/shard_map/slice | solution.py:18
  169.1 1.3 collective-permute-start.5
  170.7 1.9 collective-permute-done.5
  172.6 1.7 pad_maximum_fusion.7
  174.3 3.2 %collective-permute-start.6 = (f32[2,3,16,1,4,128]{5,2,4,3,1,0:T(8,128)}, f32[2,3,16,1,4,128]{5,2,4,3,1,0:T(8,128)}, u32[]{:S(2)}, u32[]{:S(2)}) collective-permute-start(f32[2,3,16,1,4,128]{5,2,4,3,1,0:T(8,128)} %get-tuple-element.454), channel_id=1, source_target_pairs={{0,1},{1,2},{2,3},{3,4},{4,5},{5,6},{6,7},{7,8},{8,9},{9,10},{10,1... | collective-permute-start | bytes 589832 | tf_op jit(solution)/shard_map/ppermute | solution.py:19
  177.4 1.3 collective-permute-start.7
  179.1 1.1 copy.256
  181.5 6.4 %collective-permute-done.7 = f32[2,3,16,1,4,128]{5,2,4,3,1,0:T(8,128)} collective-permute-done((f32[2,3,16,1,4,128]{5,2,4,3,1,0:T(8,128)}, f32[2,3,16,1,4,128]{5,2,4,3,1,0:T(8,128)}, u32[]{:S(2)}, u32[]{:S(2)}) %collective-permute-start.7) | collective-permute-done | bytes 196640 | tf_op jit(solution)/shard_map/ppermute | solution.py:20
  187.9 1.9 select_maximum_fusion
  192.0 39.0 %all-reduce.2 = (f32[16]{0:T(128)S(1)}, f32[16]{0:T(128)S(1)}) all-reduce(f32[16]{0:T(128)S(1)} %get-tuple-element.262, f32[16]{0:T(128)S(1)} %get-tuple-element.261), channel_id=1, replica_groups=mesh['lat'=2,'prop'=16] {'lat','prop'}, use_global_device_ids=true, to_apply=%region_10.11 | all-reduce | flops 32 | bytes 256 | tf_op jit(solution)/shard_map/psum | solution.py:166
  231.1 0.9 copy.263
  (311 shorter events, 68.2 us)
Async XLA Ops:
  0.0 23.5 %copy-start.2 = (f32[2,3,16,4,2,128]{5,4,3,2,1,0:T(2,128)S(1)}, f32[2,3,16,4,2,128]{5,4,3,2,1,0:T(2,128)}, u32[]{:S(2)}) copy-start(f32[2,3,16,4,2,128]{5,4,3,2,1,0:T(2,128)} %param.15) | copy-start | bytes 1179652
  1.2 22.2 %collective-permute-start = (f32[2,3,16,4,1,128]{5,2,4,3,1,0:T(8,128)S(1)}, f32[2,3,16,4,1,128]{5,2,4,3,1,0:T(8,128)S(1)}, u32[]{:S(2)}, u32[]{:S(2)}) collective-permute-start(f32[2,3,16,4,1,128]{5,2,4,3,1,0:T(8,128)S(1)} %get-tuple-element.468), channel_id=1, source_target_pairs={{0,16},{1,17},{2,18},{3,19},{4,20},{5,21},{6,22},{7,23},{8,24},{9,... | collective-permute-start | bytes 589832 | tf_op jit(solution)/shard_map/ppermute | solution.py:19
  6.3 14.9 %all-to-all-start = ((f32[16,1,128]{2,1,0:T(1,128)}), f32[16,1,128]{2,1,0:T(1,128)S(1)}, u32[]{:S(2)}, u32[]{:S(2)}) async-start(f32[16,1,128]{2,1,0:T(1,128)} %reshape.3988), calls=%async_computation | async-start | bytes 16384 | tf_op jit(solution)/shard_map/all_to_all | solution.py:156
  14.0 9.5 %collective-permute-start.1 = (f32[2,3,16,4,1,128]{5,2,4,3,1,0:T(8,128)S(1)}, f32[2,3,16,4,1,128]{5,2,4,3,1,0:T(8,128)S(1)}, u32[]{:S(2)}, u32[]{:S(2)}) collective-permute-start(f32[2,3,16,4,1,128]{5,2,4,3,1,0:T(8,128)S(1)} %get-tuple-element.467), channel_id=1, source_target_pairs={{16,0},{17,1},{18,2},{19,3},{20,4},{21,5},{22,6},{23,7},{24,8},{25... | collective-permute-start | bytes 589832 | tf_op jit(solution)/shard_map/ppermute | solution.py:20
  23.6 5.7 %collective-permute-start.2 = (f32[2,3,16,1,4,128]{5,2,4,3,1,0:T(8,128)S(1)}, f32[2,3,16,1,4,128]{5,2,4,3,1,0:T(8,128)S(1)}, u32[]{:S(2)}, u32[]{:S(2)}) collective-permute-start(f32[2,3,16,1,4,128]{5,2,4,3,1,0:T(8,128)S(1)} %get-tuple-element.459), channel_id=1, source_target_pairs={{0,1},{1,2},{2,3},{3,4},{4,5},{5,6},{6,7},{7,8},{8,9},{9,10},{10,1... | collective-permute-start | bytes 589832 | tf_op jit(solution)/shard_map/ppermute | solution.py:19
  26.1 8.5 %collective-permute-start.3 = (f32[2,3,16,1,4,128]{5,2,4,3,1,0:T(8,128)S(1)}, f32[2,3,16,1,4,128]{5,2,4,3,1,0:T(8,128)S(1)}, u32[]{:S(2)}, u32[]{:S(2)}) collective-permute-start(f32[2,3,16,1,4,128]{5,2,4,3,1,0:T(8,128)S(1)} %get-tuple-element.460), channel_id=1, source_target_pairs={{1,0},{2,1},{3,2},{4,3},{5,4},{6,5},{7,6},{8,7},{9,8},{10,9},{11,1... | collective-permute-start | bytes 589832 | tf_op jit(solution)/shard_map/ppermute | solution.py:20
  35.9 1.2 copy-start.9
  36.3 0.7 copy-start.4
  36.3 0.7 copy-start.6
  39.4 9.6 %copy-start.13 = (f32[4,16,16]{2,1,0:T(8,128)S(1)}, f32[4,16,16]{2,1,0:T(8,128)}, u32[]{:S(2)}) copy-start(f32[4,16,16]{2,1,0:T(8,128)} %custom-call.5) | copy-start | bytes 12292
  39.4 9.6 %copy-start.14 = (f32[4,16,16]{2,1,0:T(8,128)S(1)}, f32[4,16,16]{2,1,0:T(8,128)}, u32[]{:S(2)}) copy-start(f32[4,16,16]{2,1,0:T(8,128)} %custom-call.6) | copy-start | bytes 12292
  44.3 50.6 %all-to-all-start.1 = ((f32[16,1,6144]{2,1,0:T(1,128)}), f32[16,1,6144]{2,1,0:T(1,128)S(1)}, u32[]{:S(2)}, u32[]{:S(2)}) async-start(f32[16,1,6144]{2,1,0:T(1,128)} %reshape.3990), calls=%async_computation.1 | async-start | bytes 786432 | tf_op jit(solution)/shard_map/all_to_all | solution.py:158
  123.7 0.7 copy-start.8
  153.9 2.7 %copy-start = (f32[64,2,3,2,8,16]{5,4,3,2,1,0:T(8,128)}, f32[64,2,3,2,8,16]{5,4,3,2,1,0:T(8,128)S(1)}, u32[]{:S(2)}) copy-start(f32[64,2,3,2,8,16]{5,4,3,2,1,0:T(8,128)S(1)} %reshape.3993) | copy-start | bytes 1179652
  161.9 8.5 %copy-start.1 = (f32[2,3,16,64,2,8]{2,5,4,3,1,0:T(8,128)S(1)}, f32[2,3,16,64,2,8]{2,5,4,3,1,0:T(8,128)}, u32[]{:S(2)}) copy-start(f32[2,3,16,64,2,8]{2,5,4,3,1,0:T(8,128)} %copy.245) | copy-start | bytes 1179652
  164.6 6.2 %collective-permute-start.4 = (f32[2,3,16,4,1,128]{5,2,4,3,1,0:T(8,128)}, f32[2,3,16,4,1,128]{5,2,4,3,1,0:T(8,128)}, u32[]{:S(2)}, u32[]{:S(2)}) collective-permute-start(f32[2,3,16,4,1,128]{5,2,4,3,1,0:T(8,128)} %copy.247), channel_id=1, source_target_pairs={{0,16},{1,17},{2,18},{3,19},{4,20},{5,21},{6,22},{7,23},{8,24},{9,... | collective-permute-start | bytes 589832 | tf_op jit(solution)/shard_map/ppermute | solution.py:19
  169.1 3.5 %collective-permute-start.5 = (f32[2,3,16,4,1,128]{5,2,4,3,1,0:T(8,128)}, f32[2,3,16,4,1,128]{5,2,4,3,1,0:T(8,128)S(1)}, u32[]{:S(2)}, u32[]{:S(2)}) collective-permute-start(f32[2,3,16,4,1,128]{5,2,4,3,1,0:T(8,128)} %copy.248), channel_id=1, source_target_pairs={{16,0},{17,1},{18,2},{19,3},{20,4},{21,5},{22,6},{23,7},{24,8},{25... | collective-permute-start | bytes 589832 | tf_op jit(solution)/shard_map/ppermute | solution.py:20
  172.6 6.5 %copy-start.12 = (f32[2,3,16,4,1,128]{5,2,4,3,1,0:T(8,128)}, f32[2,3,16,4,1,128]{5,2,4,3,1,0:T(8,128)S(1)}, u32[]{:S(2)}) copy-start(f32[2,3,16,4,1,128]{5,2,4,3,1,0:T(8,128)S(1)} %collective-permute-done.5) | copy-start | bytes 589828
  174.3 7.2 %collective-permute-start.6 = (f32[2,3,16,1,4,128]{5,2,4,3,1,0:T(8,128)}, f32[2,3,16,1,4,128]{5,2,4,3,1,0:T(8,128)}, u32[]{:S(2)}, u32[]{:S(2)}) collective-permute-start(f32[2,3,16,1,4,128]{5,2,4,3,1,0:T(8,128)} %get-tuple-element.454), channel_id=1, source_target_pairs={{0,1},{1,2},{2,3},{3,4},{4,5},{5,6},{6,7},{7,8},{8,9},{9,10},{10,1... | collective-permute-start | bytes 589832 | tf_op jit(solution)/shard_map/ppermute | solution.py:19
  177.4 10.5 %collective-permute-start.7 = (f32[2,3,16,1,4,128]{5,2,4,3,1,0:T(8,128)}, f32[2,3,16,1,4,128]{5,2,4,3,1,0:T(8,128)}, u32[]{:S(2)}, u32[]{:S(2)}) collective-permute-start(f32[2,3,16,1,4,128]{5,2,4,3,1,0:T(8,128)} %get-tuple-element.455), channel_id=1, source_target_pairs={{1,0},{2,1},{3,2},{4,3},{5,4},{6,5},{7,6},{8,7},{9,8},{10,9},{11,1... | collective-permute-start | bytes 589832 | tf_op jit(solution)/shard_map/ppermute | solution.py:20
  190.4 0.9 copy-start.11
  190.4 1.0 copy-start.5
  190.4 1.1 copy-start.7
  190.5 1.3 copy-start.10
  190.5 40.5 %copy-start.3 = (f32[2,3,16,4,2,128]{5,4,3,2,1,0:T(2,128)S(1)}, f32[2,3,16,4,2,128]{5,4,3,2,1,0:T(2,128)}, u32[]{:S(2)}) copy-start(f32[2,3,16,4,2,128]{5,4,3,2,1,0:T(2,128)} %param.15) | copy-start | bytes 1179652
where the time goes:
time: 236 us; the launch traced here: 232 us
  other arithmetic  67.8 us (29%)
  local copies, waits for them, and re-layouts  57.5 us (24%)
  blocking collectives  57 us (24%)
  starting transfers between devices  27.5 us (12%)
  waiting for transfers between devices  20.7 us (9%)
    psum x1, blocking collectives, per_device(): totals = lax.psum((cross_sum, self_sum), ('lat', 'prop'))  39 us
    sub x28, other arithmetic, gain_step(): denom_imag = diag_now_imag - gain_imag  21.5 us
    sub x28, other arithmetic, gain_step(): denom_real = diag_now_real - gain_real  19.4 us
    all_to_all x1, blocking collectives, per_device(): lax.all_to_all(solved, 'prop', split_axis=3, concat_axis=5, tiled=True)  18 us
    unnamed x39, local copies, waits for them, and re-layouts  17.8 us
    ppermute x4, waiting for transfers between devices, extended(): after = lax.ppermute(first, axis, down)  13.6 us
    ppermute x4, starting transfers between devices, extended(): before = lax.ppermute(last, axis, up)  10.1 us
    all_to_all x1, starting transfers between devices, per_device(): lax.all_to_all(coeffs, 'prop', split_axis=3, concat_axis=1, tiled=True)  7.68 us
  transfers between devices with their start and end apart: 10, of which 6 were waited for; matrix products, arithmetic and copies ran while one was open for 25% of the time, Pallas kernels for 0%

commit v1 on v0

v1 whole, which is shorter than its diff:
```python
import functools

import jax
import jax.numpy as jnp
from jax import lax
from jax.experimental import pallas as pl
from jax.experimental.pallas import tpu as pltpu
from jax.sharding import PartitionSpec as P

wave_sq = 0.25
wave_shift = 0.02
loss_gain = 3.2
tiny = 1e-06
MESH = pl.DeviceIdType.MESH


def cmul(a, b):
    return (a[0] * b[0] - a[1] * b[1], a[0] * b[1] + a[1] * b[0])


def cadd(a, b):
    return (a[0] + b[0], a[1] + b[1])


def csub(a, b):
    return (a[0] - b[0], a[1] - b[1])


def cneg(a):
    return (-a[0], -a[1])


def crecip(a):
    magnitude = a[0] * a[0] + a[1] * a[1]
    return (a[0] / magnitude, -a[1] / magnitude)


def strides(size):
    found = []
    d = 1
    while d < size:
        found.append(d)
        d *= 2
    return found


def shift_y(values, step):
    shape = values.shape
    flat = values.reshape((-1, shape[-1]))
    width = shape[-1]
    lane = lax.broadcasted_iota(jnp.int32, flat.shape, 1)
    rolled = pltpu.roll(flat, (-step) % width, 1)
    keep = lane < width - 1 if step == 1 else lane > 0
    return jnp.where(keep, rolled, 0.0).reshape(shape)


def curl_part(ext, q, nz, nx):
    def at(c, dz=0, dx=0):
        return ext[q, c, 1 + dz : 1 + dz + nz, 1 + dx : 1 + dx + nx]

    ux, uy, uz = at(0), at(1), at(2)
    ux_up, ux_down = shift_y(ux, 1), shift_y(ux, -1)
    uy_down = shift_y(uy, -1)
    uz_up, uz_down = shift_y(uz, 1), shift_y(uz, -1)
    dfx_y = at(1, 0, 1) - uy
    mixed = (dfx_y - shift_y(dfx_y, -1)) + ((at(2, 0, 1) - uz) - (at(2, -1, 1) - at(2, -1)))
    out_x = (ux - ux_up) + (ux - ux_down) + (ux - at(0, 1)) + (ux - at(0, -1)) + mixed
    ux_left = at(0, 0, -1)
    uz_back = at(2, -1)
    mixed = ((ux_up - ux) - (shift_y(ux_left, 1) - ux_left)) + ((uz_up - uz) - (shift_y(uz_back, 1) - uz_back))
    out_y = (uy - at(1, 0, 1)) + (uy - at(1, 0, -1)) + (uy - at(1, 1)) + (uy - at(1, -1)) + mixed
    dfz_y = at(1, 1) - uy
    mixed = ((at(0, 1) - ux) - (at(0, 1, -1) - ux_left)) + (dfz_y - shift_y(dfz_y, -1))
    out_z = (uz - at(2, 0, 1)) + (uz - at(2, 0, -1)) + (uz - uz_up) + (uz - uz_down) + mixed
    return (out_x, out_y, out_z)


def kernel(lat_n, prop_n, total_planes, right, field, region, mask, intensity, lin, loss, kerr, out,
           ext, ext2, resid, send_f, recv_f, send_c, recv_c, edge_f, edge_c, edge_y, sums, send_sem, recv_sem):
    parts, comps, nz, nx = field.shape[:4]
    sizes = {"lat": lat_n, "prop": prop_n}
    place = {name: lax.axis_index(name) for name in sizes}
    barrier = pltpu.get_barrier_semaphore()
    expected = jnp.int32(0)
    for name, size in sizes.items():
        me = place[name]
        for d in strides(size):
            for ok, peer in ((me >= d, me - d), (me + d < size, me + d)):
                @pl.when(ok)
                def _(name=name, peer=peer):
                    pl.semaphore_signal(barrier, inc=1, device_id={name: peer}, device_id_type=MESH)
                expected = expected + ok.astype(jnp.int32)
    used = [0]
    pending = []

    def send(name, d, upward, src, dst):
        number = used[0]
        used[0] += 1
        me, size = place[name], sizes[name]
        below, above = me >= d, me + d < size
        goes, comes = (above, below) if upward else (below, above)
        peer = me + d if upward else me - d

        def copy():
            return pltpu.make_async_remote_copy(
                src_ref=src, dst_ref=dst, send_sem=send_sem.at[number], recv_sem=recv_sem.at[number],
                device_id={name: peer}, device_id_type=MESH)

        @pl.when(goes)
        def _():
            copy().start()

        pending.append((goes, copy))

        def arrive():
            @pl.when(comes)
            def _():
                copy().wait_recv()

        return arrive

    def clear(ok, ref):
        @pl.when(ok)
        def _():
            ref[...] = jnp.zeros(ref.shape, jnp.float32)

    k, j = place["prop"], place["lat"]
    first, last = k == 0, k == prop_n - 1
    clear(first, ext.at[:, :, 0, 1 : 1 + nx])
    clear(last, ext.at[:, :, nz + 1, 1 : 1 + nx])
    for target in (ext, ext2):
        clear(j == 0, target.at[:, :, :, 0])
        clear(j == lat_n - 1, target.at[:, :, :, nx + 1])
    clear(last, edge_f)
    clear(last, edge_c)
    clear(first, edge_y)
    for index, d in enumerate(strides(prop_n)):
        for side, empty in ((0, k < d), (1, k + d >= prop_n)):
            clear(empty, recv_f.at[index, side])
            clear(empty, recv_c.at[index, side])

    pl.semaphore_wait(barrier, expected)

    def swap_x(target):
        a = send("lat", 1, True, target.at[:, :, :, nx], target.at[:, :, :, 0])
        b = send("lat", 1, False, target.at[:, :, :, 1], target.at[:, :, :, nx + 1])
        return a, b

    arrive_a = send("prop", 1, True, field.at[:, :, nz - 1], ext.at[:, :, 0, 1 : 1 + nx])
    arrive_b = send("prop", 1, False, field.at[:, :, 0], ext.at[:, :, nz + 1, 1 : 1 + nx])
    for q in range(parts):
        ext[q, :, 1 : 1 + nz, 1 : 1 + nx] = field[q]

    cells = region[...]
    lin_cell = loss_cell = kerr_cell = jnp.zeros(cells.shape, jnp.float32)
    for level in range(lin.shape[0]):
        hit = cells == level
        lin_cell = jnp.where(hit, lin[level], lin_cell)
        loss_cell = jnp.where(hit, loss[level], loss_cell)
        kerr_cell = jnp.where(hit, kerr[level], kerr_cell)
    perm_real = lin_cell + mask[...].astype(jnp.float32) * kerr_cell * intensity[...]
    diag_real = 2.0 - wave_shift * perm_real
    diag_imag = (loss_gain / total_planes) * loss_cell
    diag = [(diag_real[z], diag_imag[z]) for z in range(nz)]
    inner = nz - 1
    gains = []
    for z in range(inner):
        gains.append(crecip(diag[z] if z == 0 else csub(diag[z], gains[-1])))
    low = [gains[0]]
    for z in range(1, inner):
        low.append(cmul(gains[z], low[-1]))
    for z in range(inner - 2, -1, -1):
        low[z] = cadd(low[z], cmul(gains[z], low[z + 1]))
    high = [None] * inner
    high[inner - 1] = gains[inner - 1]
    for z in range(inner - 2, -1, -1):
        high[z] = cmul(gains[z], high[z + 1])

    arrive_a()
    arrive_b()
    for arrive in swap_x(ext):
        arrive()

    def operate(source, q, curled, c):
        here = source[q, c, 1 : 1 + nz, 1 : 1 + nx]
        other = source[1 - q, c, 1 : 1 + nz, 1 : 1 + nx]
        if q == 0:
            return curled - wave_sq * (perm_real * here - loss_cell * other)
        return curled - wave_sq * (perm_real * here + loss_cell * other)

    for q in range(parts):
        curled = curl_part(ext, q, nz, nx)
        for c in range(comps):
            resid[q, c] = right[q, c] - operate(ext, q, curled[c], c)

    def res(z):
        return (resid[0, :, z], resid[1, :, z])

    locals_ = [cmul(gains[0], res(0))]
    for z in range(1, inner):
        locals_.append(cmul(gains[z], cadd(res(z), locals_[-1])))
    for z in range(inner - 2, -1, -1):
        locals_[z] = cadd(locals_[z], cmul(gains[z], locals_[z + 1]))
    steps = strides(prop_n)
    count = len(steps)
    for q in range(parts):
        send_f[count, q] = locals_[0][q]
        send_c[count, q, 0] = low[0][q]
        send_c[count, q, 1] = low[inner - 1][q]
    arrive_a = send("prop", 1, False, send_f.at[count], edge_f)
    arrive_b = send("prop", 1, False, send_c.at[count], edge_c)
    for z in range(inner):
        for q in range(parts):
            ext2[q, :, 1 + z, 1 : 1 + nx] = locals_[z][q]
    partial = cadd(res(nz - 1), locals_[inner - 1])
    arrive_a()
    arrive_b()
    inverse = crecip(csub(csub(diag[nz - 1], high[inner - 1]), (edge_c[0, 0], edge_c[1, 0])))
    below = cneg(cmul(low[inner - 1], inverse))
    above = cneg(cmul((edge_c[0, 1], edge_c[1, 1]), inverse))
    value = cmul(inverse, cadd(partial, (edge_f[0], edge_f[1])))
    for index, d in enumerate(steps):
        for q in range(parts):
            send_f[index, q] = value[q]
            send_c[index, q, 0] = below[q]
            send_c[index, q, 1] = above[q]
        arrivals = []
        for side, upward in ((0, True), (1, False)):
            arrivals.append(send("prop", d, upward, send_c.at[index], recv_c.at[index, side]))
            arrivals.append(send("prop", d, upward, send_f.at[index], recv_f.at[index, side]))
        for arrive in arrivals:
            arrive()

        def coef(side, which):
            return (recv_c[index, side, 0, which], recv_c[index, side, 1, which])

        drop = cadd(cmul(below, coef(0, 1)), cmul(above, coef(1, 0)))
        inverse = crecip((1.0 - drop[0], -drop[1]))
        lower = cmul(below, inverse)
        upper = cmul(above, inverse)
        value = csub(
            cmul(inverse, value),
            cadd(cmul(lower, (recv_f[index, 0, 0], recv_f[index, 0, 1])),
                 cmul(upper, (recv_f[index, 1, 0], recv_f[index, 1, 1]))))
        below = cneg(cmul(lower, coef(0, 0)))
        above = cneg(cmul(upper, coef(1, 1)))

    for q in range(parts):
        send_f[count + 1, q] = value[q]
        ext2[q, :, nz, 1 : 1 + nx] = value[q]
    send("prop", 1, True, send_f.at[count + 1], edge_y)()
    before = (edge_y[0], edge_y[1])
    solved = None
    for z in range(inner):
        mine = (ext2[0, :, 1 + z, 1 : 1 + nx], ext2[1, :, 1 + z, 1 : 1 + nx])
        solved = cadd(mine, cadd(cmul(low[z], before), cmul(high[z], value)))
        for q in range(parts):
            ext2[q, :, 1 + z, 1 : 1 + nx] = solved[q]
    after = csub(csub(cmul(diag[nz - 1], value), solved), res(nz - 1))
    for q in range(parts):
        ext2[q, :, 0, 1 : 1 + nx] = before[q]
        ext2[q, :, nz + 1, 1 : 1 + nx] = jnp.where(last, 0.0, after[q])
    for arrive in swap_x(ext2):
        arrive()

    cross = own = jnp.zeros(field.shape[-2:], jnp.float32)
    for q in range(parts):
        curled = curl_part(ext2, q, nz, nx)
        for c in range(comps):
            image = operate(ext2, q, curled[c], c)
            cross = cross + jnp.sum(resid[q, c] * image, axis=(0, 1))
            own = own + jnp.sum(image * image, axis=(0, 1))
    lane = lax.broadcasted_iota(jnp.int32, cross.shape, 1)
    half = cross.shape[1] // 2
    total = jnp.where(lane < half, jnp.sum(cross, axis=1, keepdims=True), jnp.sum(own, axis=1, keepdims=True))
    turn = 0
    for name, size in sizes.items():
        me = place[name]
        for d in strides(size):
            sums[turn, 0] = total
            upper_half = lax.rem(me // d, 2) == 1
            peer = jnp.where(upper_half, me - d, me + d)
            number = used[0]
            used[0] += 1
            copy = pltpu.make_async_remote_copy(
                src_ref=sums.at[turn, 0], dst_ref=sums.at[turn, 1], send_sem=send_sem.at[number],
                recv_sem=recv_sem.at[number], device_id={name: peer}, device_id_type=MESH)
            copy.start()
            copy.wait()
            total = total + sums[turn, 1]
            turn += 1
    step_size = total[:, 0:1] / (total[:, half : half + 1] + tiny)
    for q in range(parts):
        for c in range(comps):
            out[q, c] = field[q, c] + step_size * ext2[q, c, 1 : 1 + nz, 1 : 1 + nx]
    for goes, copy in pending:
        @pl.when(goes)
        def _(copy=copy):
            copy().wait_send()


def per_device(lat_n, prop_n, right_side, start_field, region, core_mask, intensity, eps_lin, eps_loss, kerr_coef):
    order = (0, 1, 3, 4, 2, 5)
    right = jnp.transpose(right_side, order)
    field = jnp.transpose(start_field, order)
    parts, comps, nz, nx, columns, ny = field.shape
    steps = len(strides(prop_n))
    turns = steps + len(strides(lat_n))
    plane = (parts, comps, nx, columns, ny)
    coefs = (parts, 2, nx, 1, ny)
    cells = (nz, nx, 1, ny)
    sem_count = 16 + 4 * steps + turns
    f32 = functools.partial(pltpu.VMEM, dtype=jnp.float32)
    vmem = pl.BlockSpec(memory_space=pltpu.VMEM)
    smem = pl.BlockSpec(memory_space=pltpu.SMEM)
    extended = (parts, comps, nz + 2, nx + 2, columns, ny)
    out = pl.pallas_call(
        functools.partial(kernel, lat_n, prop_n, nz * prop_n),
        out_shape=jax.ShapeDtypeStruct(field.shape, jnp.float32),
        in_specs=[vmem] * 5 + [smem] * 3,
        out_specs=vmem,
        scratch_shapes=[
            f32(extended), f32(extended), f32(field.shape),
            f32((steps + 2,) + plane), f32((steps, 2) + plane),
            f32((steps + 1,) + coefs), f32((steps, 2) + coefs),
            f32(plane), f32(coefs), f32(plane),
            f32((turns, 2, columns, ny)),
            pltpu.SemaphoreType.DMA((sem_count,)), pltpu.SemaphoreType.DMA((sem_count,)),
        ],
        compiler_params=pltpu.CompilerParams(collective_id=0, has_side_effects=True),
    )(right, field, region.reshape(cells), core_mask.reshape(cells), intensity.reshape(cells), eps_lin, eps_loss, kerr_coef)
    return jnp.transpose(out, (0, 1, 4, 2, 3, 5))


def solution(mesh):
    field = P(None, None, None, "prop", "lat", None)
    cell = P("prop", "lat", None)
    return jax.shard_map(
        functools.partial(per_device, mesh.shape["lat"], mesh.shape["prop"]),
        mesh=mesh,
        in_specs=(field, field, cell, cell, cell, P(), P(), P()),
        out_specs=field,
        check_vma=False,
    )
```

time: 236 us -> 63.5 us (0.27); the launches traced: 232 us -> 63.3 us
  other arithmetic: 67.8 us -> 0 us
  Pallas kernels: 0 us -> 59.2 us
  blocking collectives: 57 us -> 0 us
  local copies, waits for them, and re-layouts: 57.5 us -> 4.06 us
  starting transfers between devices: 27.5 us -> 0 us
  waiting for transfers between devices: 20.7 us -> 0 us
    pallas_call x0 -> x1, Pallas kernels: none -> 59.2 us  [per_device(): pl.pallas_call(functools.partial(kernel, lat_n, prop_n, nz * prop_n), out...]
    sub x69 -> x0, other arithmetic: 48.2 us -> none  [the longest x28 21.5 us: gain_step(): denom_imag = diag_now_imag - gain_imag]
    psum x1 -> x0, blocking collectives: 39 us -> none  [per_device(): totals = lax.psum((cross_sum, self_sum), ('lat', 'prop'))]
    all_to_all x1 -> x0, blocking collectives: 18 us -> none  [per_device(): lax.all_to_all(solved, 'prop', split_axis=3, concat_axis=5, tiled=True)]
    unnamed x39 -> x0, local copies, waits for them, and re-layouts: 17.8 us -> none
    ppermute x8 -> x0, starting transfers between devices: 15.2 us -> none  [the longest x4 10.1 us: extended(): before = lax.ppermute(last, axis, up)]
    ppermute x8 -> x0, waiting for transfers between devices: 14.8 us -> none  [the longest x4 13.6 us: extended(): after = lax.ppermute(first, axis, down)]
    all_to_all x2 -> x0, starting transfers between devices: 12.3 us -> none  [the longest x1 7.68 us: per_device(): lax.all_to_all(coeffs, 'prop', split_axis=3, concat_axis=1, tiled=True)]
  transfers between devices with their start and end apart: 10 -> 0, of which waited for: 6 -> 0; matrix products, arithmetic and copies ran while one was open for 25% -> 0% of each run, Pallas kernels for 0% -> 0%
where the time goes in v1:
time: 63.5 us; the launch traced here: 63.3 us
  Pallas kernels  59.2 us (93%)
  local copies, waits for them, and re-layouts  4.06 us (6%)
    pallas_call x1, Pallas kernels, per_device(): pl.pallas_call(functools.partial(kernel, lat_n, prop_n, nz * prop_n), out...  59.2 us
    transpose x1, local copies, waits for them, and re-layouts, per_device(): field = jnp.transpose(start_field, order)  2.11 us
    transpose x1, local copies, waits for them, and re-layouts, per_device(): return jnp.transpose(out, (0, 1, 4, 2, 3, 5))  1.94 us

profile of v1, /device:TPU:0, one launch (start us, length us, event | category | flops | bytes accessed | tf_op | source)
XLA Modules:
  0.0 63.3 jit_solution(15761875044640743370)
XLA Ops:
  0.0 2.1 %copy_bitcast_fusion = (f32[2,3,4,2,16,128]{5,4,3,2,1,0:T(8,128)}, f32[2,3,4,2,16,128]{5,4,3,2,1,0:T(8,128)}) fusion(f32[2,3,16,4,2,128]{5,4,3,2,1,0:T(2,128)} %param.9, f32[2,3,16,4,2,128]{5,4,3,2,1,0:T(2,128)} %param.8), kind=kLoop, calls=%fused_computation | loop fusion | bytes 1572864 | tf_op jit(solution)/shard_map/transpose | solution.py:305
  2.1 59.2 %shard_map.82 = f32[2,3,4,2,16,128]{5,4,3,2,1,0:T(8,128)} custom-call(f32[2,3,4,2,16,128]{5,4,3,2,1,0:T(8,128)} %get-tuple-element.6.right, f32[2,3,4,2,16,128]{5,4,3,2,1,0:T(8,128)} %get-tuple-element.5.field, s32[4,2,1,128]{3,2,1,0:T(1,128)} %bitcast.9, s32[4,2,1,128]{3,2,1,0:T(1,128)} %bitcast.10, f32[4,2,1,128]{3,2,1,0:T(1,128)} %bitcast.11, f32[8]{0:T(128)} %lin.1, ...), custom_call_target="tpu_custom_call" | custom-call | tf_op jit(solution)/shard_map/pallas_call | solution.py:317
  61.4 1.9 %copy.11 = f32[2,3,16,4,2,128]{5,4,3,2,1,0:T(2,128)} copy(f32[2,3,16,4,2,128]{5,2,4,3,1,0:T(8,128)} %bitcast.8) | data formatting | bytes 786432 | tf_op jit(solution)/shard_map/transpose | solution.py:332
